TPU v7x, 32 devices: a whole 2x2x4 slice. The times are simulated.
32 devices in a mesh: gx: 4 (over z), gy: 2 (over x), gz: 4 (over y, core).
Axes of the slice: x: 2, y: 2, z: 4, core: 2. Of those that a mesh axis runs over, the one named last changes fastest.
Arguments:
- positions: float32 [3, 16384], P(None, ('gx', 'gy', 'gz')), may hold values from -6 to 6
- frames: float32 [128, 3, 4096], P(None, None, ('gy', 'gz')), may hold values from -6 to 6
- path_slot: int32 [32, 512], P(('gx', 'gy', 'gz')), may hold values from 0 to 511, as said below
- path_count: int32 [32], replicated, may hold values from 1 to 512, 4096 in all
- path_order: int32 [4096], replicated, may hold values from 0 to 4095, each once
- frame_rank: int32 [128], replicated, may hold values from 0 to 127, each once
Outputs:
- forces: float32 [3, 16384], P(None, ('gx', 'gy', 'gz'))
- path_cv: float32 [2], replicated
Inputs may be any that keep to these rules, and one draw needn't show every extreme that they name: `path_slot`: within one domain's row the 512 local atom indices are all different.
All inputs are finite; a program needn't handle non-finite values.
Results may differ from a plain program's by a relative error of at most 0.00013.
Values sent between devices are 32-bit elements; how exact they have to be, the bound alone decides.
A program may use at most 64 MiB of HBM per device.

v0:
```python
import jax
import jax.numpy as jnp
from jax import lax
from jax.sharding import PartitionSpec as P

P_SIZE = 4096


STRENGTH = 20.0
S_HOME = 0.5
KAPPA_S = 0.5
KAPPA_Z = 0.05
PAIR_SCALE = 0.02
WIDTH_SQ = 4.0


def pair_block(block_pos, all_pos):
    diff = block_pos[:, :, None] - all_pos[:, None, :]
    dist_sq = jnp.sum(diff * diff, axis=0)
    weight = PAIR_SCALE * jnp.exp(-dist_sq / WIDTH_SQ)
    return jnp.sum(weight[None] * diff, axis=2)


def domain_forces(local):
    atoms = local.shape[1]
    rows = 256
    blocks = local.reshape(3, atoms // rows, rows).transpose(1, 0, 2)
    result = lax.map(lambda block: pair_block(block, local), blocks)
    return result.transpose(1, 0, 2).reshape(3, atoms)


def slot_ids(path_count, path_order, slots):
    offsets = jnp.cumsum(path_count) - path_count
    steps_k = jnp.arange(slots, dtype=jnp.int32)
    live = steps_k[None, :] < path_count[:, None]
    place = jnp.clip(offsets[:, None] + steps_k[None, :], 0, P_SIZE - 1)
    ids = jnp.where(live, path_order[place], -1)
    return (ids, live)


def cv_terms(dist, frame_rank):
    frames_n = dist.shape[0]
    expo = -STRENGTH * dist
    top = jnp.max(expo)
    expd = jnp.exp(expo - top)
    total = jnp.sum(expd)
    weight = expd / total
    progress_rank = frame_rank.astype(jnp.float32) / (frames_n - 1.0)
    s_value = jnp.sum(progress_rank * weight)
    z_value = -(top + jnp.log(total)) / STRENGTH
    grads = (
        KAPPA_S * P_SIZE * (s_value - S_HOME) * -STRENGTH * weight * (progress_rank - s_value)
        + KAPPA_Z * P_SIZE * z_value * weight
    )
    return (s_value, z_value, grads)


def summed_terms(partial_value, frame_rank):
    dist = lax.psum(partial_value, ("gx", "gy", "gz"))
    return cv_terms(dist, frame_rank)


def body(positions, frames, path_slot, path_count, path_order, frame_rank):
    slots = path_slot.shape[1]
    local_slot = path_slot[0]
    ids, live = slot_ids(path_count, path_order, slots)
    path_pos = jnp.take(positions, local_slot, axis=1)
    here = lax.axis_index(("gx", "gy", "gz"))
    my_ids = lax.dynamic_slice_in_dim(ids, here, 1, 0)[0]
    mask = lax.dynamic_slice_in_dim(live, here, 1, 0)[0].astype(jnp.float32)
    whole = lax.all_gather(frames, ("gy", "gz"), axis=2, tiled=True)
    refs = jnp.take(whole, jnp.clip(my_ids, 0, P_SIZE - 1), axis=2)
    delta = path_pos[None] - refs
    partial_value = jnp.sum(jnp.sum(delta * delta, axis=1) * mask[None], axis=1) / P_SIZE
    s_value, z_value, grads = summed_terms(partial_value, frame_rank)
    bias = (
        -(2.0 / P_SIZE)
        * jnp.einsum("f,fcm->cm", grads, delta, precision=lax.Precision.HIGHEST)
        * mask[None]
    )
    forces = domain_forces(positions)
    forces = forces.at[:, local_slot].add(bias)
    return (forces, jnp.stack([s_value, z_value]))


def solution(mesh):
    return jax.shard_map(
        body,
        mesh=mesh,
        in_specs=(
            P(None, ("gx", "gy", "gz")),
            P(None, None, ("gy", "gz")),
            P(("gx", "gy", "gz"), None),
            P(),
            P(),
            P(),
        ),
        out_specs=(P(None, ("gx", "gy", "gz")), P()),
        check_vma=False,
    )
```

profile of v0, /device:TPU:0, one launch (start us, length us, event | category | flops | bytes accessed | tf_op | source)
XLA Modules:
  0.0 184.7 jit_solution(5077955663486558907)
XLA Ops:
  7.2 0.7 all-gather.2.cloned.1.call-update
  7.9 0.7 copy.25
  8.8 0.7 sub.42
  9.7 90.5 %gather_fusion.1 = s32[16384]{0:T(1024)S(1)} fusion(s32[4096]{0:T(1024)S(1)} %copy-done, s32[16384]{0:T(1024)S(1)} %broadcast_clamp_fusion), kind=kCustom, calls=%fused_computation.1 | custom fusion | bytes 196608 | tf_op jit(solution)/shard_map/gather | solution.py:37
  100.2 0.1 copy.24
  100.4 1.4 while.10
  100.4 0.2 fusion.13
  100.8 0.4 fusion.14
  101.2 0.2 fusion.13
  101.5 0.4 fusion.14
  102.1 1.0 gather_fusion
  103.5 9.1 %copy.26 = f32[128,3,4096]{0,1,2:T(4,128)} copy(f32[128,3,4096]{2,0,1:T(8,128)} %all-gather.2.cloned.1.call-done) | data formatting | bytes 12582912 | tf_op jit(solution)/shard_map/all_gather | solution.py:71
  112.6 4.9 %gather_fusion.2 = f32[512,128,3]{1,2,0:T(4,128)S(1)} fusion(f32[128,3,4096]{0,1,2:T(4,128)} %copy.26, s32[1024]{0:T(1024)S(1)} %pad_clamp_fusion), kind=kCustom, calls=%fused_computation.2 | custom fusion | bytes 1574912 | tf_op jit(solution)/shard_map/jit(_take)/gather | solution.py:72
  117.5 3.0 %multiply_reduce_fusion.1 = f32[128,512]{0,1:T(8,128)S(1)} fusion(f32[512,128,3]{1,2,0:T(4,128)S(1)} %gather_fusion.2, f32[3,512]{0,1:T(8,128)S(1)} %select_bitcast_fusion, pred[512]{0:T(512)(128)(4,1)S(1)} %compare_and_fusion), kind=kLoop, calls=%fused_computation.13 | loop fusion | flops 720896 | bytes 1055232 | tf_op jit(solution)/shard_map/reduce_sum | solution.py:74
  120.4 0.1 multiply_reduce_fusion.2
  120.6 42.0 %psum.7 = f32[128]{0:T(128)S(1)} all-reduce(f32[128]{0:T(128)S(1)} %broadcast_multiply_fusion), channel_id=1, replica_groups=mesh['gx'=4,'gy'=2,'gz'=4] {'gx','gy','gz'}, use_global_device_ids=true, to_apply=%region_7.8 | all-reduce | flops 128 | bytes 1024 | tf_op jit(solution)/shard_map/psum | solution.py:59
  162.6 0.6 multiply_reduce_fusion.4
  163.2 1.3 fusion.8
  165.8 2.0 %multiply_reduce_fusion.3 = (f32[]{:T(128)}, f32[128]{0:T(128)S(1)}) fusion(s32[128]{0:T(128)S(1)} %copy-done.4, f32[]{:T(128)} %fusion.8, f32[]{:T(128)} %multiply_reduce_fusion.4, f32[128]{0:T(128)S(1)} %psum.7), kind=kLoop, calls=%fused_computation.37 | loop fusion | flops 895 | bytes 1548 | tf_op jit(solution)/shard_map/reduce_sum | solution.py:49
  168.5 0.7 multiply_add_fusion
  169.2 3.2 %multiply_reduce_fusion = f32[3,512]{0,1:T(8,128)S(1)} fusion(f32[512,128,3]{1,2,0:T(4,128)S(1)} %gather_fusion.2, f32[128]{0:T(128)S(1)} %multiply_add_fusion, f32[3,512]{0,1:T(8,128)S(1)} %select_bitcast_fusion, pred[512]{0:T(512)(128)(4,1)S(1)} %compare_and_fusion), kind=kLoop, calls=%fused_computation.12 | loop fusion | flops 784896 | bytes 799744 | tf_op jit(solution)/shard_map/f,fcm->cm/dot_general | solution.py:78
  172.4 3.5 %scatter_custom_fusion = f32[3,512]{0,1:T(8,128)S(1)} fusion(f32[3,512]{0,1:T(8,128)S(1)} %bitcast.44, s32[512]{0:T(512)S(1)} %bitcast.52, f32[3,512]{0,1:T(8,128)S(1)} %multiply_reduce_fusion, f32[512]{0:T(512)S(1)} %bitcast.46), kind=kCustom, calls=%fused_computation.14 | custom fusion | flops 3072 | bytes 270336 | tf_op jit(solution)/shard_map/scatter-add | solution.py:82
  175.9 0.7 copy.27
  176.6 1.3 pad_maximum_fusion
  (37 shorter events, 1.1 us)
Async XLA Ops:
  7.2 2.5 %copy-start = (s32[4096]{0:T(1024)S(1)}, s32[4096]{0:T(1024)}, u32[]{:S(2)}) copy-start(s32[4096]{0:T(1024)} %param.12) | copy-start | bytes 49156
  7.2 96.3 %all-gather.2.cloned.1.call-start = ((), (), s32[]{:S(2)}) async-start(), calls=%async_computation | async-start | bytes 7077888 | tf_op jit(solution)/shard_map/all_gather | solution.py:71
  9.7 90.6 %copy-start.1 = (f32[3,512]{1,0:T(4,128)S(1)}, f32[3,512]{1,0:T(4,128)}, u32[]{:S(2)}) copy-start(f32[3,512]{1,0:T(4,128)} %param.8) | copy-start | bytes 18436
  100.4 1.6 copy-start.2
  100.4 2.7 %copy-start.3 = (s32[32]{0:T(128)S(1)}, s32[32]{0:T(128)}, u32[]{:S(2)}) copy-start(s32[32]{0:T(128)} %param.11) | copy-start | bytes 388
  112.6 53.2 %copy-start.4 = (s32[128]{0:T(128)S(1)}, s32[128]{0:T(128)}, u32[]{:S(2)}) copy-start(s32[128]{0:T(128)} %param.13) | copy-start | bytes 1540
Sparse Core Ops, SparseCore 0:
  9.9 48.1 all-gather.1
where the time goes:
time: 185 us
  local copies, waits for them, and re-layouts  107 us (58%)
  blocking collectives  42 us (23%)
  other arithmetic  18.2 us (10%)
  between operations  16.3 us (9%)
    gather x2, local copies, waits for them, and re-layouts, slot_ids(): ids = jnp.where(live, path_order[place], -1)  90.5 us
    psum x1, blocking collectives, summed_terms(): dist = lax.psum(partial_value, ('gx', 'gy', 'gz'))  42 us
    all_gather x1, local copies, waits for them, and re-layouts, body(): whole = lax.all_gather(frames, ('gy', 'gz'), axis=2, tiled=True)  9.07 us
    gather x1, local copies, waits for them, and re-layouts, body(): refs = jnp.take(whole, jnp.clip(my_ids, 0, P_SIZE - 1), axis=2)  4.9 us
  transfers between devices with their start and end apart: 1, of which 0 were waited for; matrix products, arithmetic and copies ran while one was open for 52% of the time, Pallas kernels for 0%

commit v1 on v0

v1 whole, which is shorter than its diff:
```python
import functools

import jax
import jax.numpy as jnp
from jax import lax
from jax.experimental import pallas as pl
from jax.experimental.pallas import tpu as pltpu
from jax.sharding import PartitionSpec as P

STRENGTH = 20.0
S_HOME = 0.5
KAPPA_S = 0.5
KAPPA_Z = 0.05
PAIR_SCALE = 0.02
WIDTH_SQ = 4.0
LANES = 128
MESH = pl.DeviceIdType.MESH
NT = (((1,), (1,)), ((), ()))
NN = (((1,), (0,)), ((), ()))


def three_parts(x):
    high = x.astype(jnp.bfloat16).astype(jnp.float32)
    rest = x - high
    middle = rest.astype(jnp.bfloat16).astype(jnp.float32)
    return high, middle, rest - middle


def dot(a, b, dims):
    return lax.dot_general(
        a.astype(jnp.bfloat16), b.astype(jnp.bfloat16), dims, preferred_element_type=jnp.float32
    )


def iota(shape, axis):
    return lax.broadcasted_iota(jnp.int32, shape, axis)


def kernel(
    sizes, tile, cpad,
    pos_ref, frames_hbm, slot_ref, count_ref, order_ref, rank_ref,
    force_ref, cv_ref,
    frames, out1, in1, all2, all3, pair, cols, frames_sem, send1, recv1, send2, recv2, send3, recv3,
):
    nx, ny, nz = sizes
    plane = ny * nz
    n = nx * plane
    atoms = pos_ref.shape[1]
    slots = slot_ref.shape[1]
    order_rows = order_ref.shape[0]
    path = order_rows * LANES
    frames_n = frames.shape[1]
    block = frames.shape[2]
    parts = block // tile
    gx, gy, gz = lax.axis_index("gx"), lax.axis_index("gy"), lax.axis_index("gz")
    here = gy * nz + gz
    me = gx * plane + here

    def peer_of(step):
        other = lax.rem(me + step, n)
        row = lax.rem(other, plane)
        return other, (other // plane, row // nz, lax.rem(row, nz))

    def plane_peer(step):
        row = lax.rem(here + step, plane)
        return row, (gx, row // nz, lax.rem(row, nz))

    def loop(count, fn):
        lax.fori_loop(1, count, lambda step, _: (fn(step), 0)[1], 0, unroll=count <= 64)

    fetch = pltpu.make_async_copy(frames_hbm, frames, frames_sem)
    fetch.start()

    barrier = pltpu.get_barrier_semaphore()

    def greet(step):
        pl.semaphore_signal(barrier, inc=1, device_id=peer_of(step)[1], device_id_type=MESH)

    loop(n, greet)

    counts = count_ref[...]
    lane_n = iota(counts.shape, 1)
    offset = jnp.sum(jnp.where(lane_n < me, counts, 0).astype(jnp.float32), axis=1, keepdims=True).astype(jnp.int32)
    mine = jnp.sum(jnp.where(lane_n == me, counts, 0).astype(jnp.float32), axis=1, keepdims=True).astype(jnp.int32)
    k = iota((1, slots), 1)
    place = k + offset
    live_k = (k < mine).astype(jnp.float32)
    order = order_ref[...]
    table = jnp.concatenate([order // tile, lax.rem(order, tile)], axis=0).astype(jnp.float32)
    column = (iota((LANES, slots), 0) == lax.rem(place, LANES)).astype(jnp.float32)
    picked = dot(table, column, NN)
    row_hit = iota((order_rows, slots), 0) == place // LANES
    high_k = jnp.sum(jnp.where(row_hit, picked[:order_rows], 0.0), axis=0, keepdims=True)
    low_k = jnp.sum(jnp.where(row_hit, picked[order_rows:], 0.0), axis=0, keepdims=True)
    triple = jnp.concatenate(
        [high_k * live_k, low_k * live_k, live_k, jnp.zeros((5, slots), jnp.float32)], axis=0
    )
    slot_hit = (iota((atoms, slots), 0) == slot_ref[...]).astype(jnp.float32)
    per_atom = dot(triple, slot_hit, NT)
    live = per_atom[2:3]
    high = jnp.where(live > 0.5, per_atom[0:1].astype(jnp.int32), -1)
    low = per_atom[1:2].astype(jnp.int32)
    low_hit = (iota((tile, atoms), 0) == low).astype(jnp.bfloat16)

    pos = pos_ref[...]
    blocks = path // tile
    rows = blocks * cpad
    group = [pos, live]
    if cpad > 4:
        group.append(jnp.zeros((cpad - 4, atoms), jnp.float32))
    else:
        group = group * 2
    eight = jnp.concatenate(group, axis=0)
    high_hit = (iota((rows, atoms), 0) // cpad) == high
    sent = jnp.zeros((rows, tile), jnp.float32)
    for piece in three_parts(eight):
        wide = jnp.broadcast_to(piece[None], (rows // 8, 8, atoms)).reshape(rows, atoms)
        sent = sent + dot(jnp.where(high_hit, wide, 0.0), low_hit, NT)
    out1[...] = sent.reshape(plane, parts * cpad, tile)

    pl.semaphore_wait(barrier, n - 1)

    def copy1(step):
        row, device = plane_peer(step)
        return pltpu.make_async_remote_copy(
            src_ref=out1.at[row], dst_ref=in1.at[here], send_sem=send1.at[row], recv_sem=recv1.at[here],
            device_id=device, device_id_type=MESH)

    def landed1(step):
        row, device = plane_peer(step)
        pltpu.make_async_remote_copy(
            src_ref=out1.at[row], dst_ref=in1.at[row], send_sem=send1.at[row], recv_sem=recv1.at[row],
            device_id=device, device_id_type=MESH).wait_recv()

    loop(plane, lambda step: copy1(step).start())
    in1[here] = out1[here]

    height = min(32, atoms)
    padded = jnp.concatenate([pos, jnp.zeros((5, atoms), jnp.float32)], axis=0)
    cols[...] = padded.T

    def pair_step(step, totals):
        at = pl.multiple_of(step * height, height)
        source = cols[pl.ds(at, height), :]
        diffs = [pos[c:c + 1] - source[:, c:c + 1] for c in range(3)]
        dist_sq = diffs[0] * diffs[0] + diffs[1] * diffs[1] + diffs[2] * diffs[2]
        weight = PAIR_SCALE * jnp.exp(-dist_sq / WIDTH_SQ)
        return tuple(
            total + jnp.sum((weight * diff).reshape(height // 8, 8, atoms), axis=0)
            for total, diff in zip(totals, diffs)
        )

    steps = atoms // height
    first = steps // 2
    totals = lax.fori_loop(0, first, pair_step, (jnp.zeros((8, atoms), jnp.float32),) * 3)

    loop(plane, landed1)
    fetch.wait()
    known = jnp.sum(in1[...], axis=0)
    squares = jnp.zeros((frames_n, tile), jnp.float32)
    for t in range(parts):
        part = jnp.zeros((frames_n, tile), jnp.float32)
        for c in range(3):
            row = t * cpad + c
            delta = known[row:row + 1] - frames[c, :, t * tile:(t + 1) * tile]
            part = part + delta * delta
        squares = squares + part * known[t * cpad + 3:t * cpad + 4]
    all2[me] = jnp.sum(squares.T, axis=0, keepdims=True)

    def copy2(step):
        other, device = peer_of(step)
        return pltpu.make_async_remote_copy(
            src_ref=all2.at[me], dst_ref=all2.at[me], send_sem=send2.at[other], recv_sem=recv2.at[me],
            device_id=device, device_id_type=MESH)

    def landed2(step):
        other, device = peer_of(step)
        pltpu.make_async_remote_copy(
            src_ref=all2.at[other], dst_ref=all2.at[other], send_sem=send2.at[other], recv_sem=recv2.at[other],
            device_id=device, device_id_type=MESH).wait_recv()

    loop(n, lambda step: copy2(step).start())

    totals = lax.fori_loop(first, steps, pair_step, totals)
    pair[...] = jnp.concatenate([jnp.sum(total, axis=0, keepdims=True) for total in totals], axis=0)

    loop(n, landed2)
    dist = jnp.sum(all2[...], axis=0) / path
    expo = -STRENGTH * dist
    top = jnp.max(expo, axis=1, keepdims=True)
    expd = jnp.exp(expo - top)
    total = jnp.sum(expd, axis=1, keepdims=True)
    weight = expd / total
    progress = rank_ref[...].astype(jnp.float32) / (frames_n - 1.0)
    s_value = jnp.sum(progress * weight, axis=1, keepdims=True)
    z_value = -(top + jnp.log(total)) / STRENGTH
    grads = (
        KAPPA_S * path * (s_value - S_HOME) * -STRENGTH * weight * (progress - s_value)
        + KAPPA_Z * path * z_value * weight
    )
    cv_ref[...] = jnp.concatenate([s_value, z_value], axis=1)
    down = jnp.broadcast_to(grads, (tile, frames_n)).T
    moved = []
    for t in range(parts):
        for c in range(3):
            moved.append(jnp.sum(down * frames[c, :, t * tile:(t + 1) * tile], axis=0, keepdims=True))
        moved.append(jnp.zeros((cpad - 3, tile), jnp.float32))
    all3[here] = jnp.concatenate(moved, axis=0)

    def copy3(step):
        row, device = plane_peer(step)
        return pltpu.make_async_remote_copy(
            src_ref=all3.at[here], dst_ref=all3.at[here], send_sem=send3.at[row], recv_sem=recv3.at[here],
            device_id=device, device_id_type=MESH)

    def landed3(step):
        row, device = plane_peer(step)
        pltpu.make_async_remote_copy(
            src_ref=all3.at[row], dst_ref=all3.at[row], send_sem=send3.at[row], recv_sem=recv3.at[row],
            device_id=device, device_id_type=MESH).wait_recv()

    loop(plane, lambda step: copy3(step).start())
    loop(plane, lambda step: copy1(step).wait_send())
    loop(n, lambda step: copy2(step).wait_send())
    grads_sum = jnp.sum(grads, axis=1, keepdims=True)
    loop(plane, landed3)
    full = all3[...].reshape(rows, tile)
    spread = jnp.zeros((rows, atoms), jnp.float32)
    for piece in three_parts(full):
        spread = spread + dot(piece, low_hit, NN)
    chosen = jnp.sum(jnp.where(high_hit, spread, 0.0).reshape(rows // 8, 8, atoms), axis=0)
    mean_ref = chosen[0:3]
    if cpad == 4:
        mean_ref = mean_ref + chosen[4:7]
    bias = -(2.0 / path) * (grads_sum * pos - mean_ref) * live
    force_ref[...] = pair[...] + bias
    loop(plane, lambda step: copy3(step).wait_send())


def solution(mesh):
    sizes = tuple(mesh.shape[name] for name in ("gx", "gy", "gz"))

    def body(positions, frames, path_slot, path_count, path_order, frame_rank):
        plane = sizes[1] * sizes[2]
        n = sizes[0] * plane
        atoms = positions.shape[1]
        frames_n, _, block = frames.shape
        tile = min(LANES, block)
        parts = block // tile
        cpad = 4 if parts % 2 == 0 else 8
        dma = pltpu.SemaphoreType.DMA
        vmem = pl.BlockSpec(memory_space=pltpu.VMEM)
        forces, cv = pl.pallas_call(
            functools.partial(kernel, sizes, tile, cpad),
            out_shape=(
                jax.ShapeDtypeStruct((3, atoms), jnp.float32),
                jax.ShapeDtypeStruct((1, 2), jnp.float32),
            ),
            in_specs=[vmem, pl.BlockSpec(memory_space=pl.ANY), vmem, vmem, vmem, vmem],
            out_specs=(vmem, vmem),
            scratch_shapes=[
                pltpu.VMEM((3, frames_n, block), jnp.float32),
                pltpu.VMEM((plane, parts * cpad, tile), jnp.float32),
                pltpu.VMEM((plane, parts * cpad, tile), jnp.float32),
                pltpu.VMEM((n, 1, frames_n), jnp.float32),
                pltpu.VMEM((plane, parts * cpad, tile), jnp.float32),
                pltpu.VMEM((3, atoms), jnp.float32),
                pltpu.VMEM((atoms, 8), jnp.float32),
                dma,
                dma((plane,)), dma((plane,)),
                dma((n,)), dma((n,)),
                dma((plane,)), dma((plane,)),
            ],
            compiler_params=pltpu.CompilerParams(collective_id=0, has_side_effects=True),
        )(
            positions,
            jnp.transpose(frames, (1, 0, 2)),
            path_slot,
            path_count.reshape(1, n),
            path_order.reshape(-1, LANES),
            frame_rank.reshape(1, frames_n),
        )
        return forces, cv.reshape(2)

    return jax.shard_map(
        body,
        mesh=mesh,
        in_specs=(
            P(None, ("gx", "gy", "gz")),
            P(None, None, ("gy", "gz")),
            P(("gx", "gy", "gz"), None),
            P(),
            P(),
            P(),
        ),
        out_specs=(P(None, ("gx", "gy", "gz")), P()),
        check_vma=False,
    )
```

time: 185 us -> 21.8 us (0.12)
  local copies, waits for them, and re-layouts: 107 us -> 1.81 us
  blocking collectives: 42 us -> 0 us
  Pallas kernels: 0 us -> 19.2 us
  other arithmetic: 18.2 us -> 0 us
  between operations: 16.3 us -> 0.65 us
    gather x4 -> x0, local copies, waits for them, and re-layouts: 96.5 us -> none  [the longest x2 90.5 us: slot_ids(): ids = jnp.where(live, path_order[place], -1)]
    psum x1 -> x0, blocking collectives: 42 us -> none  [summed_terms(): dist = lax.psum(partial_value, ('gx', 'gy', 'gz'))]
    pallas_call x0 -> x1, Pallas kernels: none -> 19.2 us  [body(): pl.pallas_call(functools.partial(kernel, sizes, tile, cpad), out_shape=(j...]
    all_gather x1 -> x0, local copies, waits for them, and re-layouts: 9.07 us -> none  [body(): whole = lax.all_gather(frames, ('gy', 'gz'), axis=2, tiled=True)]
    reduce_sum x8 -> x0, other arithmetic: 7.49 us -> none  [the longest x1 2.95 us: body(): jnp.sum(delta * delta, axis=1) * mask[None]]
    scatter-add x1 -> x0, other arithmetic: 3.54 us -> none  [body(): forces = forces.at[:, local_slot].add(bias)]
    dot_general x1 -> x0, other arithmetic: 3.19 us -> none  [body(): jnp.einsum('f,fcm->cm', grads, delta, precision=lax.Precision.HIGHEST)]
  transfers between devices with their start and end apart: 1 -> 0, of which waited for: 0 -> 0; matrix products, arithmetic and copies ran while one was open for 52% -> 0% of each run, Pallas kernels for 0% -> 0%
where the time goes in v1:
time: 21.8 us; the launch traced here: 21.6 us
  Pallas kernels  19.2 us (88%)
  local copies, waits for them, and re-layouts  1.81 us (8%)
  between operations  0.65 us (3%)
    pallas_call x1, Pallas kernels, body(): pl.pallas_call(functools.partial(kernel, sizes, tile, cpad), out_shape=(j...  19.2 us
    unnamed x4, local copies, waits for them, and re-layouts  1.81 us

profile of v1, /device:TPU:0, one launch (start us, length us, event | category | flops | bytes accessed | tf_op | source)
XLA Modules:
  0.0 21.6 jit_solution(17389390537914177320)
XLA Ops:
  0.6 19.2 %shard_map.77 = (f32[3,512]{1,0:T(4,128)}, f32[1,2]{1,0:T(1,128)}) custom-call(f32[3,512]{1,0:T(4,128)} %pos_ref.1, f32[3,128,512]{2,1,0:T(8,128)} %bitcast.5, s32[1,512]{1,0:T(1,128)} %slot_ref.1, s32[1,32]{1,0:T(1,128)} %bitcast.7, s32[32,128]{1,0:T(8,128)} %bitcast.6, s32[1,128]{1,0:T(1,128)} %bitcast.8), custom_call_target="tpu_custom_call" | custom-call | tf_op jit(solution)/shard_map/pallas_call | solution.py:253
  19.8 0.0 copy-start
  19.8 1.3 %copy.10 = f32[3,512]{1,0:T(4,128)} copy(f32[3,512]{1,0:T(4,128)} %get-tuple-element.8) | data formatting | bytes 12288
  21.1 0.0 copy-done
  21.1 0.5 %copy.11 = f32[2]{0:T(128)} copy(f32[2]{0:T(128)S(1)} %bitcast.9) | data formatting | bytes 16
Async XLA Ops:
  19.8 1.3 %copy-start = (f32[1,2]{1,0:T(1,128)S(1)}, f32[1,2]{1,0:T(1,128)}, u32[]{:S(2)}) copy-start(f32[1,2]{1,0:T(1,128)} %get-tuple-element.5) | copy-start | bytes 28

commit v2 on v1

--- a/solution.py
+++ b/solution.py
@@ -38,9 +38,10 @@
 
 def kernel(
     sizes, tile, cpad,
-    pos_ref, frames_hbm, slot_ref, count_ref, order_ref, rank_ref,
+    pos_hbm, frames_hbm, slot_hbm, count_hbm, order_hbm, rank_hbm,
     force_ref, cv_ref,
-    frames, out1, in1, all2, all3, pair, cols, frames_sem, send1, recv1, send2, recv2, send3, recv3,
+    frames, pos_ref, slot_ref, count_ref, order_ref, rank_ref, out1, in1, all2, all3, pair, cols,
+    frames_sem, small_sem, sems1, sems2, sems3,
 ):
     nx, ny, nz = sizes
     plane = ny * nz
@@ -56,27 +57,64 @@
     here = gy * nz + gz
     me = gx * plane + here
 
-    def peer_of(step):
-        other = lax.rem(me + step, n)
-        row = lax.rem(other, plane)
-        return other, (other // plane, row // nz, lax.rem(row, nz))
-
-    def plane_peer(step):
-        row = lax.rem(here + step, plane)
-        return row, (gx, row // nz, lax.rem(row, nz))
-
-    def loop(count, fn):
-        lax.fori_loop(1, count, lambda step, _: (fn(step), 0)[1], 0, unroll=count <= 64)
+    def ring(at, size):
+        return [at] + [jnp.where(at + step >= size, at + step - size, at + step) for step in range(1, size)]
+
+    unrolled = n <= 64
+    if unrolled:
+        flat_peers = [(x, y, z) for x in ring(gx, nx) for y in ring(gy, ny) for z in ring(gz, nz)][:0:-1]
+        near_peers = [(gx, y, z) for y in ring(gy, ny) for z in ring(gz, nz)][:0:-1]
+
+    def everyone(fn):
+        if unrolled:
+            for device in flat_peers:
+                fn(device)
+            return
+
+        def visit(step, carry):
+            other = lax.rem(me + step, n)
+            row = lax.rem(other, plane)
+            fn((other // plane, row // nz, lax.rem(row, nz)))
+            return carry
+
+        lax.fori_loop(1, n, visit, 0)
+
+    def neighbours(fn):
+        if unrolled:
+            for device in near_peers:
+                fn(device)
+            return
+
+        def visit(step, carry):
+            row = lax.rem(here + step, plane)
+            fn((gx, row // nz, lax.rem(row, nz)))
+            return carry
+
+        lax.fori_loop(1, plane, visit, 0)
+
+    def send(src, dst, sems, device):
+        pltpu.make_async_remote_copy(
+            src_ref=src, dst_ref=dst, send_sem=sems.at[0], recv_sem=sems.at[1],
+            device_id=device, device_id_type=MESH).start()
+
+    def whole(ref, count, sems):
+        some = lax.rem(gx + 1, nx), gy, gz
+        part = ref.at[pl.ds(0, count)]
+        return pltpu.make_async_remote_copy(
+            src_ref=part, dst_ref=part, send_sem=sems.at[0], recv_sem=sems.at[1],
+            device_id=some, device_id_type=MESH)
 
     fetch = pltpu.make_async_copy(frames_hbm, frames, frames_sem)
+    pairs = [(pos_hbm, pos_ref), (slot_hbm, slot_ref), (count_hbm, count_ref), (order_hbm, order_ref), (rank_hbm, rank_ref)]
+    small = [pltpu.make_async_copy(src, dst, small_sem.at[i]) for i, (src, dst) in enumerate(pairs)]
+    for copy in small:
+        copy.start()
     fetch.start()
 
     barrier = pltpu.get_barrier_semaphore()
-
-    def greet(step):
-        pl.semaphore_signal(barrier, inc=1, device_id=peer_of(step)[1], device_id_type=MESH)
-
-    loop(n, greet)
+    everyone(lambda device: pl.semaphore_signal(barrier, inc=1, device_id=device, device_id_type=MESH))
+    for copy in small:
+        copy.wait()
 
     counts = count_ref[...]
     lane_n = iota(counts.shape, 1)
@@ -120,19 +158,7 @@
 
     pl.semaphore_wait(barrier, n - 1)
 
-    def copy1(step):
-        row, device = plane_peer(step)
-        return pltpu.make_async_remote_copy(
-            src_ref=out1.at[row], dst_ref=in1.at[here], send_sem=send1.at[row], recv_sem=recv1.at[here],
-            device_id=device, device_id_type=MESH)
-
-    def landed1(step):
-        row, device = plane_peer(step)
-        pltpu.make_async_remote_copy(
-            src_ref=out1.at[row], dst_ref=in1.at[row], send_sem=send1.at[row], recv_sem=recv1.at[row],
-            device_id=device, device_id_type=MESH).wait_recv()
-
-    loop(plane, lambda step: copy1(step).start())
+    neighbours(lambda device: send(out1.at[device[1] * nz + device[2]], in1.at[here], sems1, device))
     in1[here] = out1[here]
 
     height = min(32, atoms)
@@ -154,7 +180,7 @@
     first = steps // 2
     totals = lax.fori_loop(0, first, pair_step, (jnp.zeros((8, atoms), jnp.float32),) * 3)
 
-    loop(plane, landed1)
+    whole(in1, plane - 1, sems1).wait_recv()
     fetch.wait()
     known = jnp.sum(in1[...], axis=0)
     squares = jnp.zeros((frames_n, tile), jnp.float32)
@@ -167,24 +193,12 @@
         squares = squares + part * known[t * cpad + 3:t * cpad + 4]
     all2[me] = jnp.sum(squares.T, axis=0, keepdims=True)
 
-    def copy2(step):
-        other, device = peer_of(step)
-        return pltpu.make_async_remote_copy(
-            src_ref=all2.at[me], dst_ref=all2.at[me], send_sem=send2.at[other], recv_sem=recv2.at[me],
-            device_id=device, device_id_type=MESH)
-
-    def landed2(step):
-        other, device = peer_of(step)
-        pltpu.make_async_remote_copy(
-            src_ref=all2.at[other], dst_ref=all2.at[other], send_sem=send2.at[other], recv_sem=recv2.at[other],
-            device_id=device, device_id_type=MESH).wait_recv()
-
-    loop(n, lambda step: copy2(step).start())
+    everyone(lambda device: send(all2.at[me], all2.at[me], sems2, device))
 
     totals = lax.fori_loop(first, steps, pair_step, totals)
     pair[...] = jnp.concatenate([jnp.sum(total, axis=0, keepdims=True) for total in totals], axis=0)
 
-    loop(n, landed2)
+    whole(all2, n - 1, sems2).wait_recv()
     dist = jnp.sum(all2[...], axis=0) / path
     expo = -STRENGTH * dist
     top = jnp.max(expo, axis=1, keepdims=True)
@@ -200,41 +214,29 @@
     )
     cv_ref[...] = jnp.concatenate([s_value, z_value], axis=1)
     down = jnp.broadcast_to(grads, (tile, frames_n)).T
+    grads_sum = jnp.sum(grads, axis=1, keepdims=True)
     moved = []
     for t in range(parts):
         for c in range(3):
-            moved.append(jnp.sum(down * frames[c, :, t * tile:(t + 1) * tile], axis=0, keepdims=True))
+            pulled = jnp.sum(down * frames[c, :, t * tile:(t + 1) * tile], axis=0, keepdims=True)
+            row = t * cpad + c
+            moved.append(-(2.0 / path) * (grads_sum * known[row:row + 1] - pulled))
         moved.append(jnp.zeros((cpad - 3, tile), jnp.float32))
     all3[here] = jnp.concatenate(moved, axis=0)
-
-    def copy3(step):
-        row, device = plane_peer(step)
-        return pltpu.make_async_remote_copy(
-            src_ref=all3.at[here], dst_ref=all3.at[here], send_sem=send3.at[row], recv_sem=recv3.at[here],
-            device_id=device, device_id_type=MESH)
-
-    def landed3(step):
-        row, device = plane_peer(step)
-        pltpu.make_async_remote_copy(
-            src_ref=all3.at[row], dst_ref=all3.at[row], send_sem=send3.at[row], recv_sem=recv3.at[row],
-            device_id=device, device_id_type=MESH).wait_recv()
-
-    loop(plane, lambda step: copy3(step).start())
-    loop(plane, lambda step: copy1(step).wait_send())
-    loop(n, lambda step: copy2(step).wait_send())
-    grads_sum = jnp.sum(grads, axis=1, keepdims=True)
-    loop(plane, landed3)
+    neighbours(lambda device: send(all3.at[here], all3.at[here], sems3, device))
+    whole(in1, plane - 1, sems1).wait_send()
+    whole(all2, n - 1, sems2).wait_send()
+    whole(all3, plane - 1, sems3).wait_recv()
     full = all3[...].reshape(rows, tile)
     spread = jnp.zeros((rows, atoms), jnp.float32)
     for piece in three_parts(full):
         spread = spread + dot(piece, low_hit, NN)
     chosen = jnp.sum(jnp.where(high_hit, spread, 0.0).reshape(rows // 8, 8, atoms), axis=0)
-    mean_ref = chosen[0:3]
+    bias = chosen[0:3]
     if cpad == 4:
-        mean_ref = mean_ref + chosen[4:7]
-    bias = -(2.0 / path) * (grads_sum * pos - mean_ref) * live
+        bias = bias + chosen[4:7]
     force_ref[...] = pair[...] + bias
-    loop(plane, lambda step: copy3(step).wait_send())
+    whole(all3, plane - 1, sems3).wait_send()
 
 
 def solution(mesh):
@@ -253,23 +255,25 @@
         forces, cv = pl.pallas_call(
             functools.partial(kernel, sizes, tile, cpad),
             out_shape=(
-                jax.ShapeDtypeStruct((3, atoms), jnp.float32),
-                jax.ShapeDtypeStruct((1, 2), jnp.float32),
+                pltpu.VMEM((3, atoms), jnp.float32),
+                pltpu.VMEM((1, 2), jnp.float32),
             ),
-            in_specs=[vmem, pl.BlockSpec(memory_space=pl.ANY), vmem, vmem, vmem, vmem],
+            in_specs=[pl.BlockSpec(memory_space=pl.ANY)] * 6,
             out_specs=(vmem, vmem),
             scratch_shapes=[
                 pltpu.VMEM((3, frames_n, block), jnp.float32),
+                pltpu.VMEM((3, atoms), jnp.float32),
+                pltpu.VMEM((1, path_slot.shape[1]), jnp.int32),
+                pltpu.VMEM((1, n), jnp.int32),
+                pltpu.VMEM((path_order.shape[0] // LANES, LANES), jnp.int32),
+                pltpu.VMEM((1, frames_n), jnp.int32),
                 pltpu.VMEM((plane, parts * cpad, tile), jnp.float32),
                 pltpu.VMEM((plane, parts * cpad, tile), jnp.float32),
                 pltpu.VMEM((n, 1, frames_n), jnp.float32),
                 pltpu.VMEM((plane, parts * cpad, tile), jnp.float32),
                 pltpu.VMEM((3, atoms), jnp.float32),
                 pltpu.VMEM((atoms, 8), jnp.float32),
-                dma,
-                dma((plane,)), dma((plane,)),
-                dma((n,)), dma((n,)),
-                dma((plane,)), dma((plane,)),
+                dma, dma((5,)), dma((2,)), dma((2,)), dma((2,)),
             ],
             compiler_params=pltpu.CompilerParams(collective_id=0, has_side_effects=True),
         )(

time: 21.8 us -> 19.6 us (0.90)
  Pallas kernels: 19.2 us -> 17.6 us
  local copies, waits for them, and re-layouts: 1.81 us -> 1.11 us
    pallas_call x1, Pallas kernels: 19.2 us -> 17.6 us  [body(): pl.pallas_call(functools.partial(kernel, sizes, tile, cpad), out_shape=(p...]
    unnamed x4 -> x2, local copies, waits for them, and re-layouts: 1.81 us -> 1.11 us
where the time goes in v2:
time: 19.6 us; the launch traced here: 19.3 us
  Pallas kernels  17.6 us (90%)
  local copies, waits for them, and re-layouts  1.11 us (6%)
  between operations  0.64 us (3%)
    pallas_call x1, Pallas kernels, body(): pl.pallas_call(functools.partial(kernel, sizes, tile, cpad), out_shape=(p...  17.6 us
    unnamed x2, local copies, waits for them, and re-layouts  1.11 us

profile of v2, /device:TPU:0, one launch (start us, length us, event | category | flops | bytes accessed | tf_op | source)
XLA Modules:
  0.0 19.3 jit_solution(5287574113541611191)
XLA Ops:
  0.6 17.6 %shard_map.77 = (f32[3,512]{1,0:T(4,128)S(1)}, f32[1,2]{1,0:T(1,128)S(1)}) custom-call(f32[3,512]{1,0:T(4,128)} %pos_hbm.1, f32[3,128,512]{2,1,0:T(8,128)} %bitcast.6, s32[1,512]{1,0:T(1,128)} %slot_hbm.1, s32[1,32]{1,0:T(1,128)} %bitcast.8, s32[32,128]{1,0:T(8,128)} %bitcast.7, s32[1,128]{1,0:T(1,128)} %bitcast.9), custom_call_target="tpu_custom_call" | custom-call | tf_op jit(solution)/shard_map/pallas_call | solution.py:255
  18.2 0.6 %copy.10 = f32[3,512]{1,0:T(4,128)} copy(f32[3,512]{1,0:T(4,128)S(1)} %get-tuple-element.6) | data formatting | bytes 12288
  18.8 0.5 %copy.11 = f32[2]{0:T(128)} copy(f32[2]{0:T(128)S(1)} %bitcast.5) | data formatting | bytes 16
